TPU v7x, 32 devices: a whole 2x2x4 slice. The times are simulated.
32 devices in a mesh: wide: 16 (over z, y, x), narrow: 2 (over core).
Axes of the slice: x: 2, y: 2, z: 4, core: 2. Of those that a mesh axis runs over, the one named last changes fastest.
Arguments:
- positions: float32 [3, 8192], P(None, ('wide', 'narrow')), may hold values from 0 to 1
- forces: float32 [3, 16, 8192], P(None, None, ('wide', 'narrow')), may hold values from -6 to 6
- waves: int32 [3, 8192], replicated, may hold values from -16 to 16, as said below
Outputs:
- velocity: float32 [3, 16, 8192], P(None, None, ('wide', 'narrow'))
Inputs may be any that keep to these rules, and one draw needn't show every extreme that they name: `waves`: no wavevector is (0, 0, 0).
All inputs are finite; a program needn't handle non-finite values.
Results may differ from a plain program's by a relative error of at most 0.0053.
Values may be sent and summed in bfloat16 or wider, within the bound.
No kernel may reach another device: no remote copies, remote signals or barrier semaphores. Data moves between devices by JAX's collectives and lax.ppermute only.
A program may use at most 64 MiB of HBM per device.

v0:
```python
import jax
import jax.numpy as jnp
from jax import lax
from jax.sharding import PartitionSpec as P

two_pi = 6.283185307179586
radius = 0.005
xi_split = 40.0


def make_tables(wblock, positions):
    mf = wblock.astype(jnp.float32)
    theta = two_pi * (
        mf[0][:, None] * positions[0][None, :]
        + mf[1][:, None] * positions[1][None, :]
        + mf[2][:, None] * positions[2][None, :]
    )
    return (jnp.cos(theta).astype(jnp.bfloat16), jnp.sin(theta).astype(jnp.bfloat16))


def scale_sums(sums, wblock, amp):
    cols = sums.shape[1]
    split = sums.reshape(2, 3, -1, cols)
    kvec = two_pi * wblock.astype(jnp.float32)
    ksq = jnp.sum(kvec * kvec, axis=0)
    inner = jnp.sum(kvec[None, :, None, :] * split, axis=1)
    proj = split - kvec[None, :, None, :] * (inner / ksq)[:, None, :, :]
    qarg = ksq / (4.0 * xi_split * xi_split)
    factor = (
        amp
        * (1.0 - radius * radius * ksq / 3.0)
        * (1.0 + qarg + 2.0 * qarg * qarg)
        * jnp.exp(-qarg)
        / ksq
    )
    return (proj * factor).reshape(sums.shape[0], cols).astype(jnp.bfloat16)


def shards(positions, forces, waves):
    rows = positions.shape[1]
    kwaves = waves.shape[1]
    devices = lax.axis_size("wide") * lax.axis_size("narrow")
    force_bf = forces.reshape(-1, rows).astype(jnp.bfloat16)
    half = force_bf.shape[0]
    width = 256
    dims = (((1,), (1,)), ((), ()))
    cos_table, sin_table = make_tables(waves, positions)
    sum_cos = lax.dot_general(force_bf, cos_table, dims, preferred_element_type=jnp.float32)
    sum_sin = lax.dot_general(force_bf, sin_table, dims, preferred_element_type=jnp.float32)
    terms = jnp.concatenate([sum_cos, sum_sin], axis=0)
    amp = 20000.0 / jnp.sqrt(jnp.float32(rows * devices) * jnp.float32(kwaves))

    def apply_block(total, piece, begin, cols):
        cosine = lax.dynamic_slice_in_dim(cos_table, begin, cols, 0)
        sine = lax.dynamic_slice_in_dim(sin_table, begin, cols, 0)
        total = total + jnp.dot(piece[:half], cosine, preferred_element_type=jnp.float32)
        return total + jnp.dot(piece[half:], sine, preferred_element_type=jnp.float32)

    empty = jnp.zeros((half, rows), jnp.float32)
    owned = lax.psum_scatter(terms, ("wide", "narrow"), scatter_dimension=1, tiled=True)
    cols = owned.shape[1]
    wblock = lax.dynamic_slice_in_dim(waves, lax.axis_index(("wide", "narrow")) * cols, cols, 1)
    scaled = scale_sums(owned, wblock, amp)
    piece = lax.all_gather(scaled, ("wide", "narrow"), axis=1, tiled=True)
    cols = piece.shape[1]

    def inner(step, acc):
        sub = lax.dynamic_slice_in_dim(piece, step * width, width, 1)
        return apply_block(acc, sub, step * width, width)

    total = lax.fori_loop(0, cols // width, inner, empty)
    return total.reshape(forces.shape)


def solution(mesh):
    placed = (P(None, ("wide", "narrow")), P(None, None, ("wide", "narrow")), P())
    return jax.shard_map(
        shards,
        mesh=mesh,
        in_specs=placed,
        out_specs=P(None, None, ("wide", "narrow")),
        check_vma=False,
    )
```

profile of v0, /device:TPU:0, one launch (start us, length us, event | category | flops | bytes accessed | tf_op | source)
XLA Modules:
  0.0 309.1 jit_solution(3159215597644270184)
XLA Ops:
  9.2 29.7 %convolution_bitcast_fusion.1 = f32[48,8192]{1,0:T(8,128)S(1)} fusion(bf16[48,256]{1,0:T(8,128)(2,1)S(1)} %bitcast.35, f32[256]{0:T(256)S(1)} %bitcast.40, f32[8192]{0:T(1024)S(1)} %bitcast.29, f32[256]{0:T(256)S(1)} %bitcast.43, f32[8192]{0:T(1024)S(1)} %bitcast.32, f32[256]{0:T(256)S(1)} %bitcast.37, f32[8192]{0:T(1024)S(1)} %bitcast.26), kind=kOutput, calls=%fused_computation.9 | convolution fusion | flops 216006656 | bytes 1698816 | tf_op jit(solution)/shard_map/dot_general | solution.py:48
  38.9 30.4 %convolution_bitcast_fusion = f32[48,8192]{1,0:T(8,128)S(1)} fusion(bf16[48,256]{1,0:T(8,128)(2,1)S(1)} %bitcast.36, f32[256]{0:T(256)S(1)} %bitcast.41, f32[8192]{0:T(1024)S(1)} %bitcast.30, f32[256]{0:T(256)S(1)} %bitcast.44, f32[8192]{0:T(1024)S(1)} %bitcast.33, f32[256]{0:T(256)S(1)} %bitcast.38, f32[8192]{0:T(1024)S(1)} %bitcast.27), kind=kOutput, calls=%fused_computation.8 | convolution fusion | flops 216006656 | bytes 1698816 | tf_op jit(solution)/shard_map/dot_general | solution.py:49
  69.3 1.9 pad_maximum_fusion
  72.0 104.2 %reduce-scatter.2.cloned.1.call-done = f32[96,256]{1,0:T(8,128)} async-done(((f32[96,8192]{1,0:T(8,128)}), f32[96,256]{1,0:T(8,128)}) %reduce-scatter.2.cloned.1.call-update) | async-done | bytes 98320 | tf_op jit(solution)/shard_map/reduce_scatter | solution.py:60
  177.1 1.5 fusion.7
  178.7 34.2 %sine_convert_fusion = (bf16[8192,256]{1,0:T(8,128)(2,1)}, bf16[8192,256]{1,0:T(8,128)(2,1)}) fusion(f32[256]{0:T(256)S(1)} %bitcast.42, f32[8192]{0:T(1024)S(1)} %bitcast.31, f32[256]{0:T(256)S(1)} %bitcast.45, f32[8192]{0:T(1024)S(1)} %bitcast.34, f32[256]{0:T(256)S(1)} %bitcast.39, f32[8192]{0:T(1024)S(1)} %bitcast.28), kind=kLoop, calls=%fused_computation.10 | loop fusion | flops 16777216 | bytes 8489984 | tf_op jit(solution)/shard_map/convert_element_type | solution.py:18
  212.9 19.7 %all-gather.2.cloned.1.call-done = bf16[96,8192]{1,0:T(8,128)(2,1)} async-done(((bf16[96,256]{1,0:T(8,128)(2,1)}), bf16[96,8192]{1,0:T(8,128)(2,1)}) %all-gather.2.cloned.1.call-update) | async-done | bytes 1572880 | tf_op jit(solution)/shard_map/all_gather | solution.py:64
  232.6 69.0 %while.14 = (s32[]{:T(128)}, f32[48,256]{1,0:T(8,128)S(1)}, bf16[96,8192]{1,0:T(8,128)(2,1)}, bf16[8192,256]{1,0:T(8,128)(2,1)}, bf16[8192,256]{1,0:T(8,128)(2,1...) while((s32[]{:T(128)}, f32[48,256]{1,0:T(8,128)S(1)}, bf16[96,8192]{1,0:T(8,128)(2,1)}, ...), condition=%wide.region_4.0_spmd.clone, body=%wide.region_3.0_spmd.clone.sunk | while | flops 12619784 | bytes 511144 | solution.py:71
  234.8 1.1 convolution_add_fusion.4
  236.9 1.1 convolution_add_fusion.4
  239.1 1.1 convolution_add_fusion.4
  241.2 1.1 convolution_add_fusion.4
  243.4 1.1 convolution_add_fusion.4
  245.5 1.1 convolution_add_fusion.4
  247.7 1.1 convolution_add_fusion.4
  252.0 1.1 convolution_add_fusion.4
  256.3 1.1 convolution_add_fusion.4
  258.5 1.1 convolution_add_fusion.4
  260.6 1.1 convolution_add_fusion.4
  262.8 1.1 convolution_add_fusion.4
  264.9 1.1 convolution_add_fusion.4
  267.1 1.1 convolution_add_fusion.4
  269.3 1.1 convolution_add_fusion.4
  271.4 1.1 convolution_add_fusion.4
  273.6 1.1 convolution_add_fusion.4
  275.7 1.1 convolution_add_fusion.4
  280.0 1.1 convolution_add_fusion.4
  284.3 1.1 convolution_add_fusion.4
  288.7 1.1 convolution_add_fusion.4
  293.0 1.1 convolution_add_fusion.4
  297.3 1.1 convolution_add_fusion.4
  299.4 1.1 convolution_add_fusion.4
  (56 shorter events, 48.0 us)
Async XLA Ops:
  6.5 169.6 %reduce-scatter.2.cloned.1.call-start = ((), (), s32[]{:S(2)}) async-start(), calls=%async_computation.1 | async-start | bytes 3244032 | tf_op jit(solution)/shard_map/reduce_scatter | solution.py:60
  71.2 161.4 %all-gather.2.cloned.1.call-start = ((), (), s32[]{:S(2)}) async-start(), calls=%async_computation.2 | async-start | bytes 1622016 | tf_op jit(solution)/shard_map/all_gather | solution.py:64
  301.6 0.6 copy-start
Sparse Core Ops, SparseCore 0:
  71.3 104.8 reduce-scatter.1
  179.0 53.5 all-gather.1
where the time goes:
time: 311 us; the launch traced here: 309 us
  matrix products  129 us (41%)
  waiting for transfers between devices  124 us (40%)
  other arithmetic  41 us (13%)
  between operations  13.5 us (4%)
    reduce_scatter x1, waiting for transfers between devices, shards(): lax.psum_scatter(terms, ('wide', 'narrow'), scatter_dimension=1, tiled=True)  104 us
    dot_general x32, matrix products, apply_block(): jnp.dot(piece[:half], cosine, preferred_element_type=jnp.float32)  34.5 us
    dot_general x32, matrix products, apply_block(): jnp.dot(piece[half:], sine, preferred_element_type=jnp.float32)  34.5 us
    convert_element_type x1, other arithmetic, make_tables(): jnp.sin(theta).astype(jnp.bfloat16)  34.2 us
    dot_general x1, matrix products, shards(): lax.dot_general(force_bf, sin_table, dims, preferred_element_type=jnp.flo...  30.4 us
    dot_general x1, matrix products, shards(): lax.dot_general(force_bf, cos_table, dims, preferred_element_type=jnp.flo...  29.7 us
    all_gather x1, waiting for transfers between devices, shards(): piece = lax.all_gather(scaled, ('wide', 'narrow'), axis=1, tiled=True)  19.7 us
  transfers between devices with their start and end apart: 2, of which 2 were waited for; matrix products, arithmetic and copies ran while one was open for 11% of the time, Pallas kernels for 0%

commit v1 on v0

--- a/solution.py
+++ b/solution.py
@@ -61,7 +61,8 @@
     cols = owned.shape[1]
     wblock = lax.dynamic_slice_in_dim(waves, lax.axis_index(("wide", "narrow")) * cols, cols, 1)
     scaled = scale_sums(owned, wblock, amp)
-    piece = lax.all_gather(scaled, ("wide", "narrow"), axis=1, tiled=True)
+    sent = jnp.stack([scaled] * lax.axis_size(("wide", "narrow")))
+    piece = jnp.concatenate(lax.all_to_all(sent, ("wide", "narrow"), 0, 0), axis=1)
     cols = piece.shape[1]
 
     def inner(step, acc):

time: 311 us -> 298 us (0.958)
  waiting for transfers between devices: 124 us -> 108 us
  starting transfers between devices: 0.04 us -> 3.71 us
    all_gather x1 -> x0, waiting for transfers between devices: 19.7 us -> none  [shards(): piece = lax.all_gather(scaled, ('wide', 'narrow'), axis=1, tiled=True)]
    all_to_all x0 -> x1, starting transfers between devices: none -> 3.71 us  [shards(): lax.all_to_all(sent, ('wide', 'narrow'), 0, 0)]
    all_to_all x0 -> x1, waiting for transfers between devices: none -> 3.43 us  [shards(): lax.all_to_all(sent, ('wide', 'narrow'), 0, 0)]
  transfers between devices with their start and end apart: 2 -> 2, of which waited for: 2 -> 2; matrix products, arithmetic and copies ran while one was open for 11% -> 12% of each run, Pallas kernels for 0% -> 0%
where the time goes in v1:
time: 298 us; the launch traced here: 296 us
  matrix products  128 us (43%)
  waiting for transfers between devices  108 us (36%)
  other arithmetic  40.4 us (14%)
  between operations  13.5 us (5%)
  starting transfers between devices  3.71 us (1%)
  local copies, waits for them, and re-layouts  3.04 us (1%)
    reduce_scatter x1, waiting for transfers between devices, shards(): lax.psum_scatter(terms, ('wide', 'narrow'), scatter_dimension=1, tiled=True)  104 us
    convert_element_type x1, other arithmetic, make_tables(): jnp.sin(theta).astype(jnp.bfloat16)  34.2 us
    dot_general x32, matrix products, apply_block(): jnp.dot(piece[:half], cosine, preferred_element_type=jnp.float32)  34 us
    dot_general x32, matrix products, apply_block(): jnp.dot(piece[half:], sine, preferred_element_type=jnp.float32)  33.9 us
    dot_general x1, matrix products, shards(): lax.dot_general(force_bf, sin_table, dims, preferred_element_type=jnp.flo...  30.4 us
    dot_general x1, matrix products, shards(): lax.dot_general(force_bf, cos_table, dims, preferred_element_type=jnp.flo...  29.7 us
  transfers between devices with their start and end apart: 2, of which 2 were waited for; matrix products, arithmetic and copies ran while one was open for 12% of the time, Pallas kernels for 0%

profile of v1, /device:TPU:0, one launch (start us, length us, event | category | flops | bytes accessed | tf_op | source)
XLA Modules:
  0.0 296.4 jit_solution(6948155403430265434)
XLA Ops:
  9.2 29.7 %convolution_bitcast_fusion.1 = f32[48,8192]{1,0:T(8,128)S(1)} fusion(bf16[48,256]{1,0:T(8,128)(2,1)S(1)} %bitcast.40, f32[256]{0:T(256)S(1)} %bitcast.45, f32[8192]{0:T(1024)S(1)} %bitcast.34, f32[256]{0:T(256)S(1)} %bitcast.48, f32[8192]{0:T(1024)S(1)} %bitcast.37, f32[256]{0:T(256)S(1)} %bitcast.42, f32[8192]{0:T(1024)S(1)} %bitcast.31), kind=kOutput, calls=%fused_computation.9 | convolution fusion | flops 216006656 | bytes 1698816 | tf_op jit(solution)/shard_map/dot_general | solution.py:48
  38.9 30.4 %convolution_bitcast_fusion = f32[48,8192]{1,0:T(8,128)S(1)} fusion(bf16[48,256]{1,0:T(8,128)(2,1)S(1)} %bitcast.41, f32[256]{0:T(256)S(1)} %bitcast.46, f32[8192]{0:T(1024)S(1)} %bitcast.35, f32[256]{0:T(256)S(1)} %bitcast.49, f32[8192]{0:T(1024)S(1)} %bitcast.38, f32[256]{0:T(256)S(1)} %bitcast.43, f32[8192]{0:T(1024)S(1)} %bitcast.32), kind=kOutput, calls=%fused_computation.8 | convolution fusion | flops 216006656 | bytes 1698816 | tf_op jit(solution)/shard_map/dot_general | solution.py:49
  69.3 1.9 pad_maximum_fusion
  71.9 104.3 %reduce-scatter.2.cloned.1.call-done = f32[96,256]{1,0:T(8,128)} async-done(((f32[96,8192]{1,0:T(8,128)}), f32[96,256]{1,0:T(8,128)}) %reduce-scatter.2.cloned.1.call-update) | async-done | bytes 98320 | tf_op jit(solution)/shard_map/reduce_scatter | solution.py:60
  178.1 1.4 stack.2
  179.5 3.7 %all-to-all-start = ((bf16[32,96,256]{2,1,0:T(8,128)(2,1)}), bf16[32,96,256]{2,1,0:T(8,128)(2,1)S(1)}, u32[]{:S(2)}, u32[]{:S(2)}) async-start(bf16[32,96,256]{2,1,0:T(8,128)(2,1)} %stack.2), calls=%async_computation.1 | async-start | bytes 3145728 | tf_op jit(solution)/shard_map/all_to_all | solution.py:65
  183.2 34.2 %sine_convert_fusion = (bf16[8192,256]{1,0:T(8,128)(2,1)}, bf16[8192,256]{1,0:T(8,128)(2,1)}) fusion(f32[256]{0:T(256)S(1)} %bitcast.47, f32[8192]{0:T(1024)S(1)} %bitcast.36, f32[256]{0:T(256)S(1)} %bitcast.50, f32[8192]{0:T(1024)S(1)} %bitcast.39, f32[256]{0:T(256)S(1)} %bitcast.44, f32[8192]{0:T(1024)S(1)} %bitcast.33), kind=kLoop, calls=%fused_computation.10 | loop fusion | flops 16777216 | bytes 8489984 | tf_op jit(solution)/shard_map/convert_element_type | solution.py:18
  217.4 3.4 %all-to-all-done = bf16[32,96,256]{2,1,0:T(8,128)(2,1)S(1)} async-done(((bf16[32,96,256]{2,1,0:T(8,128)(2,1)}), bf16[32,96,256]{2,1,0:T(8,128)(2,1)S(1)}, u32[]{:S(2)}, u32[]{:S(2)}) %all-to-all-start) | async-done | bytes 1572896 | tf_op jit(solution)/shard_map/all_to_all | solution.py:65
  221.0 67.9 %while.14 = (s32[]{:T(128)}, f32[48,256]{1,0:T(8,128)S(1)}, bf16[96,8192]{1,0:T(8,128)(2,1)S(1)}, bf16[8192,256]{1,0:T(8,128)(2,1)}, bf16[8192,256]{1,0:T(8,128)...) while((s32[]{:T(128)}, f32[48,256]{1,0:T(8,128)S(1)}, ...), condition=%wide.region_4.0_spmd.clone, body=%wide.region_3.0_spmd.clone.sunk | while | flops 12619784 | bytes 511144 | solution.py:72
  225.2 1.1 convolution_add_fusion.4
  227.3 1.1 convolution_add_fusion.4
  231.6 1.1 convolution_add_fusion.4
  233.7 1.1 convolution_add_fusion.4
  235.8 1.1 convolution_add_fusion.4
  240.1 1.1 convolution_add_fusion.4
  242.2 1.1 convolution_add_fusion.4
  244.3 1.1 convolution_add_fusion.4
  248.6 1.1 convolution_add_fusion.4
  250.7 1.1 convolution_add_fusion.4
  252.8 1.1 convolution_add_fusion.4
  257.0 1.1 convolution_add_fusion.4
  259.2 1.1 convolution_add_fusion.4
  261.3 1.1 convolution_add_fusion.4
  265.5 1.1 convolution_add_fusion.4
  267.6 1.1 convolution_add_fusion.4
  269.8 1.1 convolution_add_fusion.4
  274.0 1.1 convolution_add_fusion.4
  276.1 1.1 convolution_add_fusion.4
  278.3 1.1 convolution_add_fusion.4
  282.5 1.1 convolution_add_fusion.4
  284.6 1.1 convolution_add_fusion.4
  286.8 1.1 convolution_add_fusion.4
  (57 shorter events, 49.4 us)
Async XLA Ops:
  6.5 169.7 %reduce-scatter.2.cloned.1.call-start = ((), (), s32[]{:S(2)}) async-start(), calls=%async_computation.2 | async-start | bytes 3244032 | tf_op jit(solution)/shard_map/reduce_scatter | solution.py:60
  179.5 41.4 %all-to-all-start = ((bf16[32,96,256]{2,1,0:T(8,128)(2,1)}), bf16[32,96,256]{2,1,0:T(8,128)(2,1)S(1)}, u32[]{:S(2)}, u32[]{:S(2)}) async-start(bf16[32,96,256]{2,1,0:T(8,128)(2,1)} %stack.2), calls=%async_computation.1 | async-start | bytes 3145728 | tf_op jit(solution)/shard_map/all_to_all | solution.py:65
  288.9 0.6 copy-start
Sparse Core Ops, SparseCore 0:
  71.3 104.8 reduce-scatter.1
